TPU v7x, 32 devices: a whole 2x2x4 slice. The times are simulated.
32 devices in a mesh: rep: 4 (over z), dp: 2 (over x), ctx: 4 (over y, core).
Axes of the slice: x: 2, y: 2, z: 4, core: 2. Of those that a mesh axis runs over, the one named last changes fastest.
Arguments:
- hidden_in: bfloat16 [8, 2048, 2048], P(('rep', 'dp'), 'ctx'), may hold values from -6 to 6
- segments: int32 [8, 2048], P(('rep', 'dp'), 'ctx'), may hold values from -1 to 31, as said below
- cotangent: bfloat16 [8, 2048, 2048], P(('rep', 'dp'), 'ctx'), may hold values from -6 to 6
- attn_gain: float32 [2048], P(('dp', 'ctx')), may hold values from 0.25 to 1.75
- w_query: float32 [2048, 2048], P(('dp', 'ctx')), may hold values from -0.125 to 0.125
- key_projection: float32 [2048, 1024], P(('dp', 'ctx')), may hold values from -0.125 to 0.125
- value_projection: float32 [2048, 1024], P(('dp', 'ctx')), may hold values from -0.125 to 0.125
- q_gain: float32 [128], P(('dp', 'ctx')), may hold values from 1 to 2.5
- k_gain: float32 [128], P(('dp', 'ctx')), may hold values from 0.25 to 1.75
- w_gate: float32 [2048, 16], P(('dp', 'ctx')), may hold values from -0.25 to 0.25
- w_out: float32 [2048, 2048], P(('dp', 'ctx')), may hold values from -1 to 1
- mlp_gain: float32 [2048], P(('dp', 'ctx')), may hold values from 0.25 to 1.75
- w_gate_ff: float32 [2048, 6144], P(('dp', 'ctx')), may hold values from -0.125 to 0.125
- w_up: float32 [2048, 6144], P(('dp', 'ctx')), may hold values from -0.125 to 0.125
- w_down: float32 [6144, 2048], P(('dp', 'ctx')), may hold values from -0.078125 to 0.078125
Outputs:
- layer_out: bfloat16 [8, 2048, 2048], P(('rep', 'dp'), 'ctx')
- input_grad: bfloat16 [8, 2048, 2048], P(('rep', 'dp'), 'ctx')
- grad_attn_gain: float32 [2048], P(('dp', 'ctx'))
- grad_query: float32 [2048, 2048], P(('dp', 'ctx'))
- grad_key: float32 [2048, 1024], P(('dp', 'ctx'))
- grad_value: float32 [2048, 1024], P(('dp', 'ctx'))
- grad_q_gain: float32 [128], P(('dp', 'ctx'))
- grad_k_gain: float32 [128], P(('dp', 'ctx'))
- grad_gate: float32 [2048, 16], P(('dp', 'ctx'))
- grad_out: float32 [2048, 2048], P(('dp', 'ctx'))
- grad_mlp_gain: float32 [2048], P(('dp', 'ctx'))
- grad_gate_ff: float32 [2048, 6144], P(('dp', 'ctx'))
- grad_up: float32 [2048, 6144], P(('dp', 'ctx'))
- grad_down: float32 [6144, 2048], P(('dp', 'ctx'))
Inputs may be any that keep to these rules, and one draw needn't show every extreme that they name: `segments`: in each sequence the ids number its 32 documents from 0 at the first token and rise by one at each document's start until the padding; the first document holds at least 768 tokens; every sequence ends with 1 to 256 padding tokens marked -1.
All inputs are finite; a program needn't handle non-finite values.
Results may differ from a plain program's by a relative error of at most 0.02.
The roundings to bfloat16 on the way count: a program that leaves them out, or rounds other values in their place, can miss the bound.
Values may be sent and summed in bfloat16 or wider, within the bound.
No kernel may reach another device: no remote copies, remote signals or barrier semaphores. Data moves between devices by JAX's collectives and lax.ppermute only.
A program may use at most 448 MiB of HBM per device.

v0:
```python
import jax
import jax.numpy as jnp
from jax import lax
from jax.sharding import PartitionSpec as P

QUERY_HEADS = 16
KEY_VALUE_HEADS = 8
HEAD_SIZE = 128


epsilon = 1e-06
masked_score = -1e30


def inverse_root(value):
    return lax.rsqrt(jnp.mean(value * value, axis=-1, keepdims=True) + epsilon)


def norm_pullback(grad_in, normed_rows, inverse, gain):
    scaled = grad_in * gain
    return inverse * (scaled - normed_rows * jnp.mean(normed_rows * scaled, axis=-1, keepdims=True))


def matrix_product(left, right):
    return jnp.dot(left, right, preferred_element_type=jnp.float32)


def outer_sum(left, right):
    return lax.dot_general(
        left, right, (((0,), (0,)), ((), ())), preferred_element_type=jnp.float32
    )


def through_rows(left, right):
    return lax.dot_general(
        left, right, (((1,), (1,)), ((), ())), preferred_element_type=jnp.float32
    )


def allowed_mask(seg_query, seg_keys, offset):
    spot_query = offset + jnp.arange(seg_query.shape[1])
    spot_keys = jnp.arange(seg_keys.shape[1])
    same = (
        (seg_query[:, :, None] == seg_keys[:, None, :])
        & (seg_query[:, :, None] >= 0)
        & (spot_keys[None, None, :] <= spot_query[None, :, None])
    )
    return same | (spot_keys[None, None, :] == spot_query[None, :, None])


def body(
    hidden_in,
    segments,
    cotangent,
    attn_gain,
    w_query,
    key_projection,
    value_projection,
    q_gain,
    k_gain,
    w_gate,
    w_out,
    mlp_gain,
    w_gate_ff,
    w_up,
    w_down,
):
    packed_sequences, shard_local_rows, model_dim = hidden_in.shape
    token_rows = packed_sequences * shard_local_rows
    query_group = QUERY_HEADS // KEY_VALUE_HEADS
    scale = HEAD_SIZE ** (-0.5)
    brain_float_half = jnp.bfloat16
    f32 = jnp.float32
    shard_ga = attn_gain.astype(brain_float_half)
    shard_wq = w_query.astype(brain_float_half)
    shard_wk = key_projection.astype(brain_float_half)
    shard_wv = value_projection.astype(brain_float_half)
    shard_gq = q_gain.astype(brain_float_half)
    shard_gk = k_gain.astype(brain_float_half)
    shard_wa = w_gate.astype(brain_float_half)
    shard_wo = w_out.astype(brain_float_half)
    shard_gm = mlp_gain.astype(brain_float_half)
    shard_wg = w_gate_ff.astype(brain_float_half)
    shard_wu = w_up.astype(brain_float_half)
    shard_wd = w_down.astype(brain_float_half)
    attention_params = (
        lax.all_gather(shard_ga, ("dp", "ctx"), axis=0, tiled=True),
        lax.all_gather(shard_wq, ("dp", "ctx"), axis=0, tiled=True),
        lax.all_gather(shard_wk, ("dp", "ctx"), axis=0, tiled=True),
        lax.all_gather(shard_wv, ("dp", "ctx"), axis=0, tiled=True),
        lax.all_gather(shard_gq, ("dp", "ctx"), axis=0, tiled=True),
        lax.all_gather(shard_gk, ("dp", "ctx"), axis=0, tiled=True),
        lax.all_gather(shard_wa, ("dp", "ctx"), axis=0, tiled=True),
        lax.all_gather(shard_wo, ("dp", "ctx"), axis=0, tiled=True),
    )
    mlp_set = (
        lax.all_gather(shard_gm, ("dp", "ctx"), axis=0, tiled=True),
        lax.all_gather(shard_wg, ("dp", "ctx"), axis=0, tiled=True),
        lax.all_gather(shard_wu, ("dp", "ctx"), axis=0, tiled=True),
        lax.all_gather(shard_wd, ("dp", "ctx"), axis=0, tiled=True),
    )
    x_rows = hidden_in.reshape(token_rows, model_dim).astype(f32)
    inverse_a = inverse_root(x_rows)
    normed_a = x_rows * inverse_a
    gain_a = attention_params[0].astype(f32)
    normed_input = (normed_a * gain_a).astype(brain_float_half)
    queries = matrix_product(normed_input, attention_params[1]).reshape(
        token_rows, QUERY_HEADS, HEAD_SIZE
    )
    unnormed_keys = matrix_product(normed_input, attention_params[2]).reshape(
        token_rows, KEY_VALUE_HEADS, HEAD_SIZE
    )
    value_half = matrix_product(normed_input, attention_params[3]).astype(brain_float_half)
    logits = matrix_product(normed_input, attention_params[6])
    gain_q = attention_params[4].astype(f32)
    key_gain_vector = attention_params[5].astype(f32)
    inverse_q = inverse_root(queries)
    normed_q = queries * inverse_q
    query_norm_layer = (normed_q * gain_q).astype(brain_float_half)
    key_inverse_norm = inverse_root(unnormed_keys)
    normed_key_rows = unnormed_keys * key_inverse_norm
    key_norm_layer = (normed_key_rows * key_gain_vector).astype(brain_float_half)
    key_row_block = key_norm_layer.reshape(
        packed_sequences, shard_local_rows, KEY_VALUE_HEADS * HEAD_SIZE
    )
    value_row_block = value_half.reshape(
        packed_sequences, shard_local_rows, KEY_VALUE_HEADS * HEAD_SIZE
    )
    key_value_params = (
        lax.all_gather(key_row_block, "ctx", axis=1, tiled=True),
        lax.all_gather(value_row_block, "ctx", axis=1, tiled=True),
        lax.all_gather(segments, "ctx", axis=1, tiled=True),
    )
    offset = lax.axis_index("ctx") * shard_local_rows
    key_count_total = key_value_params[0].shape[1]
    allowed = allowed_mask(segments, key_value_params[2], offset)
    query_head_rows = query_norm_layer.reshape(
        packed_sequences, shard_local_rows, KEY_VALUE_HEADS, query_group, HEAD_SIZE
    ).transpose(2, 0, 1, 3, 4)
    key_head_rows = (
        key_value_params[0]
        .reshape(packed_sequences, key_count_total, KEY_VALUE_HEADS, HEAD_SIZE)
        .transpose(2, 0, 1, 3)
    )
    value_head_rows = (
        key_value_params[1]
        .reshape(packed_sequences, key_count_total, KEY_VALUE_HEADS, HEAD_SIZE)
        .transpose(2, 0, 1, 3)
    )

    def head_forward(inputs):
        q_part, k_part, v_part = inputs
        scores = jnp.einsum("sqgd,std->sgqt", q_part, k_part, preferred_element_type=f32) * scale
        scores = jnp.where(allowed[:, None], scores, masked_score)
        peak = jnp.max(scores, axis=-1, keepdims=True)
        expon = jnp.exp(scores - peak)
        summed = jnp.sum(expon, axis=-1, keepdims=True)
        probs = (expon / summed).astype(brain_float_half)
        mixed = jnp.einsum("sgqt,std->sqgd", probs, v_part, preferred_element_type=f32)
        return (mixed, (peak + jnp.log(summed))[..., 0])

    head_out, log_norm = lax.map(head_forward, (query_head_rows, key_head_rows, value_head_rows))
    mixed_heads = head_out.transpose(1, 2, 0, 3, 4).reshape(token_rows, QUERY_HEADS, HEAD_SIZE)
    gate_sig = jax.nn.sigmoid(logits)
    gated = (
        (mixed_heads * gate_sig[:, :, None])
        .reshape(token_rows, QUERY_HEADS * HEAD_SIZE)
        .astype(brain_float_half)
    )
    middle = x_rows + matrix_product(gated, attention_params[7])
    inverse_m = inverse_root(middle)
    normed_m = middle * inverse_m
    gain_m = mlp_set[0].astype(f32)
    normed_mid = (normed_m * gain_m).astype(brain_float_half)
    gate_ff = matrix_product(normed_mid, mlp_set[1])
    up_ff = matrix_product(normed_mid, mlp_set[2])
    sig_ff = jax.nn.sigmoid(gate_ff)
    hidden_b = (gate_ff * sig_ff * up_ff).astype(brain_float_half)
    result = middle + matrix_product(hidden_b, mlp_set[3])
    layer_out = result.astype(brain_float_half).reshape(
        packed_sequences, shard_local_rows, model_dim
    )
    valid = (segments.reshape(token_rows, 1) >= 0).astype(f32)
    grad_y = cotangent.reshape(token_rows, model_dim).astype(f32) * valid
    grad_yb = grad_y.astype(brain_float_half)
    grad_down_term = outer_sum(hidden_b, grad_yb)
    grad_hidden = through_rows(grad_yb, mlp_set[3])
    grad_gate_b = (grad_hidden * up_ff * sig_ff * (1.0 + gate_ff * (1.0 - sig_ff))).astype(
        brain_float_half
    )
    grad_up_b = (grad_hidden * gate_ff * sig_ff).astype(brain_float_half)
    grad_gateff_term = outer_sum(normed_mid, grad_gate_b)
    grad_up_term = outer_sum(normed_mid, grad_up_b)
    grad_normed_m = through_rows(grad_gate_b, mlp_set[1]) + through_rows(grad_up_b, mlp_set[2])
    grad_gm_term = jnp.sum(grad_normed_m * normed_m, axis=0)
    grad_middle = grad_y + norm_pullback(grad_normed_m, normed_m, inverse_m, gain_m)
    mlp_shares = (
        lax.psum_scatter(
            grad_gm_term.astype(jnp.bfloat16), ("dp", "ctx"), scatter_dimension=0, tiled=True
        ).astype(jnp.float32),
        lax.psum_scatter(
            grad_gateff_term.astype(jnp.bfloat16), ("dp", "ctx"), scatter_dimension=0, tiled=True
        ).astype(jnp.float32),
        lax.psum_scatter(
            grad_up_term.astype(jnp.bfloat16), ("dp", "ctx"), scatter_dimension=0, tiled=True
        ).astype(jnp.float32),
        lax.psum_scatter(
            grad_down_term.astype(jnp.bfloat16), ("dp", "ctx"), scatter_dimension=0, tiled=True
        ).astype(jnp.float32),
    )
    grad_middle_b = grad_middle.astype(brain_float_half)
    grad_wo_term = outer_sum(gated, grad_middle_b)
    grad_gated = through_rows(grad_middle_b, attention_params[7]).reshape(
        token_rows, QUERY_HEADS, HEAD_SIZE
    )
    grad_sig = jnp.sum(grad_gated * mixed_heads, axis=-1)
    grad_logits = (grad_sig * gate_sig * (1.0 - gate_sig)).astype(brain_float_half)
    mixed_gradient_rows = (grad_gated * gate_sig[:, :, None]).astype(brain_float_half)
    grad_wa_term = outer_sum(normed_input, grad_logits)
    allowed_back = allowed_mask(segments, key_value_params[2], offset)
    key_pullback = (
        key_value_params[0]
        .reshape(packed_sequences, key_count_total, KEY_VALUE_HEADS, HEAD_SIZE)
        .transpose(2, 0, 1, 3)
    )
    value_pullback = (
        key_value_params[1]
        .reshape(packed_sequences, key_count_total, KEY_VALUE_HEADS, HEAD_SIZE)
        .transpose(2, 0, 1, 3)
    )
    head_gradient_rows = mixed_gradient_rows.reshape(
        packed_sequences, shard_local_rows, KEY_VALUE_HEADS, query_group, HEAD_SIZE
    ).transpose(2, 0, 1, 3, 4)

    def head_backward(inputs):
        q_part, k_part, v_part, grad_part, norm_part = inputs
        scores = jnp.einsum("sqgd,std->sgqt", q_part, k_part, preferred_element_type=f32) * scale
        probs = jnp.where(allowed_back[:, None], jnp.exp(scores - norm_part[..., None]), 0.0)
        grad_value = jnp.einsum(
            "sgqt,sqgd->std", probs.astype(brain_float_half), grad_part, preferred_element_type=f32
        )
        grad_probs = jnp.einsum("sqgd,std->sgqt", grad_part, v_part, preferred_element_type=f32)
        inner = jnp.sum(probs * grad_probs, axis=-1, keepdims=True)
        grad_scores = (probs * (grad_probs - inner)).astype(brain_float_half)
        grad_query = (
            jnp.einsum("sgqt,std->sqgd", grad_scores, k_part, preferred_element_type=f32) * scale
        )
        grad_key = (
            jnp.einsum("sgqt,sqgd->std", grad_scores, q_part, preferred_element_type=f32) * scale
        )
        return (grad_query, grad_key, grad_value)

    head_dq, head_key_gradient, head_value_gradient = lax.map(
        head_backward, (query_head_rows, key_pullback, value_pullback, head_gradient_rows, log_norm)
    )
    grad_qn = head_dq.transpose(1, 2, 0, 3, 4).reshape(token_rows, QUERY_HEADS, HEAD_SIZE)
    key_gradient_total = head_key_gradient.transpose(1, 2, 0, 3).reshape(
        packed_sequences, key_count_total, KEY_VALUE_HEADS * HEAD_SIZE
    )
    value_gradient_total = head_value_gradient.transpose(1, 2, 0, 3).reshape(
        packed_sequences, key_count_total, KEY_VALUE_HEADS * HEAD_SIZE
    )
    key_reverse_pass, value_reverse_pass = (
        lax.psum_scatter(
            key_gradient_total.astype(jnp.bfloat16), "ctx", scatter_dimension=1, tiled=True
        ).astype(jnp.float32),
        lax.psum_scatter(
            value_gradient_total.astype(jnp.bfloat16), "ctx", scatter_dimension=1, tiled=True
        ).astype(jnp.float32),
    )
    normed_key_gradient = key_reverse_pass.reshape(token_rows, KEY_VALUE_HEADS, HEAD_SIZE)
    value_gradient_half = value_reverse_pass.reshape(
        token_rows, KEY_VALUE_HEADS * HEAD_SIZE
    ).astype(brain_float_half)
    grad_gq_term = jnp.sum(grad_qn * normed_q, axis=(0, 1))
    grad_gk_term = jnp.sum(normed_key_gradient * normed_key_rows, axis=(0, 1))
    grad_query_b = (
        norm_pullback(grad_qn, normed_q, inverse_q, gain_q)
        .astype(brain_float_half)
        .reshape(token_rows, QUERY_HEADS * HEAD_SIZE)
    )
    grad_key_b = (
        norm_pullback(normed_key_gradient, normed_key_rows, key_inverse_norm, key_gain_vector)
        .astype(brain_float_half)
        .reshape(token_rows, KEY_VALUE_HEADS * HEAD_SIZE)
    )
    grad_wq_term = outer_sum(normed_input, grad_query_b)
    grad_wk_term = outer_sum(normed_input, grad_key_b)
    grad_wv_term = outer_sum(normed_input, value_gradient_half)
    grad_normed_a = (
        through_rows(grad_query_b, attention_params[1])
        + through_rows(grad_key_b, attention_params[2])
        + through_rows(value_gradient_half, attention_params[3])
        + through_rows(grad_logits, attention_params[6])
    )
    grad_ga_term = jnp.sum(grad_normed_a * normed_a, axis=0)
    input_grad = (
        (grad_middle + norm_pullback(grad_normed_a, normed_a, inverse_a, gain_a))
        .astype(brain_float_half)
        .reshape(packed_sequences, shard_local_rows, model_dim)
    )
    attn_shares = (
        lax.psum_scatter(
            grad_ga_term.astype(jnp.bfloat16), ("dp", "ctx"), scatter_dimension=0, tiled=True
        ).astype(jnp.float32),
        lax.psum_scatter(
            grad_wq_term.astype(jnp.bfloat16), ("dp", "ctx"), scatter_dimension=0, tiled=True
        ).astype(jnp.float32),
        lax.psum_scatter(
            grad_wk_term.astype(jnp.bfloat16), ("dp", "ctx"), scatter_dimension=0, tiled=True
        ).astype(jnp.float32),
        lax.psum_scatter(
            grad_wv_term.astype(jnp.bfloat16), ("dp", "ctx"), scatter_dimension=0, tiled=True
        ).astype(jnp.float32),
        lax.psum_scatter(
            grad_gq_term.astype(jnp.bfloat16), ("dp", "ctx"), scatter_dimension=0, tiled=True
        ).astype(jnp.float32),
        lax.psum_scatter(
            grad_gk_term.astype(jnp.bfloat16), ("dp", "ctx"), scatter_dimension=0, tiled=True
        ).astype(jnp.float32),
        lax.psum_scatter(
            grad_wa_term.astype(jnp.bfloat16), ("dp", "ctx"), scatter_dimension=0, tiled=True
        ).astype(jnp.float32),
        lax.psum_scatter(
            grad_wo_term.astype(jnp.bfloat16), ("dp", "ctx"), scatter_dimension=0, tiled=True
        ).astype(jnp.float32),
    )
    totals = (
        lax.psum(attn_shares[0].astype(jnp.bfloat16), "rep").astype(jnp.float32),
        lax.psum(attn_shares[1].astype(jnp.bfloat16), "rep").astype(jnp.float32),
        lax.psum(attn_shares[2].astype(jnp.bfloat16), "rep").astype(jnp.float32),
        lax.psum(attn_shares[3].astype(jnp.bfloat16), "rep").astype(jnp.float32),
        lax.psum(attn_shares[4].astype(jnp.bfloat16), "rep").astype(jnp.float32),
        lax.psum(attn_shares[5].astype(jnp.bfloat16), "rep").astype(jnp.float32),
        lax.psum(attn_shares[6].astype(jnp.bfloat16), "rep").astype(jnp.float32),
        lax.psum(attn_shares[7].astype(jnp.bfloat16), "rep").astype(jnp.float32),
        lax.psum(mlp_shares[0].astype(jnp.bfloat16), "rep").astype(jnp.float32),
        lax.psum(mlp_shares[1].astype(jnp.bfloat16), "rep").astype(jnp.float32),
        lax.psum(mlp_shares[2].astype(jnp.bfloat16), "rep").astype(jnp.float32),
        lax.psum(mlp_shares[3].astype(jnp.bfloat16), "rep").astype(jnp.float32),
    )
    return (layer_out, input_grad) + tuple(totals)


def solution(mesh):
    placed = (
        P(("rep", "dp"), "ctx", None),
        P(("rep", "dp"), "ctx"),
        P(("rep", "dp"), "ctx", None),
        P(("dp", "ctx")),
        P(("dp", "ctx"), None),
        P(("dp", "ctx"), None),
        P(("dp", "ctx"), None),
        P(("dp", "ctx")),
        P(("dp", "ctx")),
        P(("dp", "ctx"), None),
        P(("dp", "ctx"), None),
        P(("dp", "ctx")),
        P(("dp", "ctx"), None),
        P(("dp", "ctx"), None),
        P(("dp", "ctx"), None),
    )
    return jax.shard_map(
        body,
        mesh=mesh,
        in_specs=placed,
        out_specs=(
            P(("rep", "dp"), "ctx", None),
            P(("rep", "dp"), "ctx", None),
            P(("dp", "ctx")),
            P(("dp", "ctx"), None),
            P(("dp", "ctx"), None),
            P(("dp", "ctx"), None),
            P(("dp", "ctx")),
            P(("dp", "ctx")),
            P(("dp", "ctx"), None),
            P(("dp", "ctx"), None),
            P(("dp", "ctx")),
            P(("dp", "ctx"), None),
            P(("dp", "ctx"), None),
            P(("dp", "ctx"), None),
        ),
        check_vma=False,
    )
```

profile of v0, /device:TPU:0, one launch (start us, length us, event | category | flops | bytes accessed | tf_op | source)
XLA Modules:
  0.0 2281.4 jit_solution(16184878322409342712)
XLA Ops:
  22.6 27.3 %all-gather.13.cloned.1.call-done = bf16[2048,1024]{1,0:T(8,128)(2,1)} async-done(((bf16[256,1024]{1,0:T(8,128)(2,1)}), bf16[2048,1024]{1,0:T(8,128)(2,1)}) %all-gather.13.cloned.1.call-update) | async-done | bytes 4194320 | tf_op jit(solution)/shard_map/all_gather | solution.py:90
  169.2 50.1 %all-gather.19.cloned.1.call-done = bf16[2048,2048]{1,0:T(8,128)(2,1)} async-done(((bf16[256,2048]{1,0:T(8,128)(2,1)}), bf16[2048,2048]{1,0:T(8,128)(2,1)}) %all-gather.19.cloned.1.call-update) | async-done | bytes 8388624 | tf_op jit(solution)/shard_map/all_gather | solution.py:88
  249.6 93.1 %while.28 = (s32[]{:T(128)}, f32[8,1,512,2,128]{2,4,3,1,0:T(8,128)}, f32[8,1,2,512]{3,2,1,0:T(2,128)}, bf16[8,1,2048,128]{3,2,1,0:T(8,128)(2,1)}, bf16[8,1,2048,...) while((s32[]{:T(128)}, ...), condition=%wide.region_6.7_spmd.clone, body=%wide.region_3.6_spmd.clone.sunk | while | flops 1105198080 | bytes 31242872 | solution.py:162
  357.1 46.8 %all-gather.23.cloned.1.call-done = bf16[2048,6144]{1,0:T(8,128)(2,1)} async-done(((bf16[256,6144]{1,0:T(8,128)(2,1)}), bf16[2048,6144]{1,0:T(8,128)(2,1)}) %all-gather.23.cloned.1.call-update) | async-done | bytes 25165840 | tf_op jit(solution)/shard_map/all_gather | solution.py:98
  403.9 21.0 fusion.135
  424.9 106.8 %all-gather.25.cloned.1.call-done = bf16[2048,6144]{1,0:T(8,128)(2,1)} async-done(((bf16[256,6144]{1,0:T(8,128)(2,1)}), bf16[2048,6144]{1,0:T(8,128)(2,1)}) %all-gather.25.cloned.1.call-update) | async-done | bytes 25165840 | tf_op jit(solution)/shard_map/all_gather | solution.py:99
  531.7 20.5 fusion.136
  552.2 107.3 %all-gather.27.cloned.1.call-done = bf16[6144,2048]{1,0:T(8,128)(2,1)} async-done(((bf16[768,2048]{1,0:T(8,128)(2,1)}), bf16[6144,2048]{1,0:T(8,128)(2,1)}) %all-gather.27.cloned.1.call-update) | async-done | bytes 25165840 | tf_op jit(solution)/shard_map/all_gather | solution.py:100
  659.5 30.4 %multiply_convert_fusion = (bf16[512,6144]{1,0:T(8,128)(2,1)}, bf16[512,6144]{1,0:T(8,128)(2,1)}, bf16[512,6144]{1,0:T(8,128)(2,1)}) fusion(f32[512,6144]{1,0:T(8,128)} %fusion.135, f32[512,6144]{1,0:T(8,128)} %fusion.136, bf16[6144,2048]{1,0:T(8,128)(2,1)} %all-gather.27.cloned.1.call-done, bf16[1,512,2048]{2,1,0:T(8,128)(2,1)} %param.21, ...), kind=kOutput, calls=%fused_computation.82 | convolution fusion | flops 12938379264 | bytes 71305216 | tf_op jit(solution)/shard_map/dot_general | solution.py:35
  690.0 21.1 fusion.137
  711.1 21.1 multiply_reduce_fusion
  757.5 196.7 %while.29 = (s32[]{:T(128)}, f32[8,1,512,2,128]{2,4,3,1,0:T(8,128)}, bf16[8,1,2048,128]{2,3,0,1:T(8,128)(2,1)}, bf16[8,1,2048,128]{2,3,0,1:T(8,128)(2,1)}, bf16[...) while((s32[]{:T(128)}, ...), condition=%wide.region_11.12_spmd.clone, body=%wide.region_9.11_spmd.clone.sunk | while | flops 2722757632 | bytes 124302064 | solution.py:253
  1010.0 36.2 %reduce-scatter.13.cloned.1.call-done = bf16[1,512,1024]{1,2,0:T(8,128)(2,1)} async-done(((bf16[1,2048,1024]{1,2,0:T(8,128)(2,1)}), bf16[1,512,1024]{1,2,0:T(8,128)(2,1)}) %reduce-scatter.13.cloned.1.call-update) | async-done | bytes 1048592 | tf_op jit(solution)/shard_map/reduce_scatter | solution.py:267
  1052.0 20.7 convolution_convert_fusion.2
  1073.2 21.4 convolution_convert_fusion.1
  1095.3 20.9 convolution_convert_fusion
  1128.1 67.9 %reduce-scatter.23.cloned.1.call-done = bf16[256,2048]{1,0:T(8,128)(2,1)} async-done(((bf16[2048,2048]{1,0:T(8,128)(2,1)}), bf16[256,2048]{1,0:T(8,128)(2,1)}) %reduce-scatter.23.cloned.1.call-update) | async-done | bytes 1048592 | tf_op jit(solution)/shard_map/reduce_scatter | solution.py:324
  1196.0 54.6 %reduce-scatter.17.cloned.1.call-done = bf16[256,1024]{1,0:T(8,128)(2,1)} async-done(((bf16[2048,1024]{1,0:T(8,128)(2,1)}), bf16[256,1024]{1,0:T(8,128)(2,1)}) %reduce-scatter.17.cloned.1.call-update) | async-done | bytes 524304 | tf_op jit(solution)/shard_map/reduce_scatter | solution.py:309
  1250.5 55.0 %reduce-scatter.19.cloned.1.call-done = bf16[256,1024]{1,0:T(8,128)(2,1)} async-done(((bf16[2048,1024]{1,0:T(8,128)(2,1)}), bf16[256,1024]{1,0:T(8,128)(2,1)}) %reduce-scatter.19.cloned.1.call-update) | async-done | bytes 524304 | tf_op jit(solution)/shard_map/reduce_scatter | solution.py:312
  1305.5 160.4 %reduce-scatter.25.cloned.1.call-done = bf16[256,6144]{1,0:T(8,128)(2,1)} async-done(((bf16[2048,6144]{1,0:T(8,128)(2,1)}), bf16[256,6144]{1,0:T(8,128)(2,1)}) %reduce-scatter.25.cloned.1.call-update) | async-done | bytes 3145744 | tf_op jit(solution)/shard_map/reduce_scatter | solution.py:201
  1465.9 160.4 %reduce-scatter.27.cloned.1.call-done = bf16[256,6144]{1,0:T(8,128)(2,1)} async-done(((bf16[2048,6144]{1,0:T(8,128)(2,1)}), bf16[256,6144]{1,0:T(8,128)(2,1)}) %reduce-scatter.27.cloned.1.call-update) | async-done | bytes 3145744 | tf_op jit(solution)/shard_map/reduce_scatter | solution.py:204
  1626.2 160.4 %reduce-scatter.29.cloned.1.call-done = bf16[768,2048]{1,0:T(8,128)(2,1)} async-done(((bf16[6144,2048]{1,0:T(8,128)(2,1)}), bf16[768,2048]{1,0:T(8,128)(2,1)}) %reduce-scatter.29.cloned.1.call-update) | async-done | bytes 3145744 | tf_op jit(solution)/shard_map/reduce_scatter | solution.py:207
  1798.7 20.8 fusion.97
  1873.0 383.0 %all-reduce.12.cloned.1.call-done = (bf16[256,2048]{1,0:T(8,128)(2,1)}, bf16[256,1024]{1,0:T(8,128)(2,1)}, bf16[256,1024]{1,0:T(8,128)(2,1)}, bf16[256,2048]{1,0...) async-done(((bf16[256,2048]{1,0:T(8,128)(2,1)}, bf16[256,1024]{1,0:T(8,128)(2,1)}, bf16[256,1024]{1,0:T(8,128)(2,1)}, ...) | async-done | bytes 12582928 | tf_op jit(solution)/shard_map/psum | solution.py:330
  (438 shorter events, 648.9 us)
Async XLA Ops:
  7.2 42.7 %all-gather.13.cloned.1.call-start = ((), (), s32[]{:S(2)}) async-start(), calls=%async_computation.10 | async-start | bytes 4718592 | tf_op jit(solution)/shard_map/all_gather | solution.py:90
  9.5 79.9 %all-gather.15.cloned.1.call-start = ((), (), s32[]{:S(2)}) async-start(), calls=%async_computation.11 | async-start | bytes 4718592 | tf_op jit(solution)/shard_map/all_gather | solution.py:89
  11.7 137.3 %all-gather.29.cloned.1.call-start = ((), (), s32[]{:S(2)}) async-start(), calls=%async_computation.28 | async-start | bytes 5242880 | tf_op jit(solution)/shard_map/all_gather | solution.py:131
  22.1 209.6 %copy-start.42 = (f32[8,1,256]{2,1,0:T(1,128)}, f32[8,1,256]{2,1,0:T(1,128)S(1)}, u32[]{:S(2)}) copy-start(f32[8,1,256]{2,1,0:T(1,128)S(1)} %convert_element_type.362) | copy-start | bytes 24580
  22.6 209.1 %copy-start.46 = (f32[512]{0:T(512)}, f32[512]{0:T(512)S(1)}, u32[]{:S(2)}) copy-start(f32[512]{0:T(512)S(1)} %add_rsqrt_fusion.3) | copy-start | bytes 6148
  55.5 107.0 %all-gather.17.cloned.1.call-start = ((), (), s32[]{:S(2)}) async-start(), calls=%async_computation.12 | async-start | bytes 5242880 | tf_op jit(solution)/shard_map/all_gather | solution.py:130
  103.4 115.9 %all-gather.19.cloned.1.call-start = ((), (), s32[]{:S(2)}) async-start(), calls=%async_computation.13 | async-start | bytes 9437184 | tf_op jit(solution)/shard_map/all_gather | solution.py:88
  106.2 240.7 %all-gather.21.cloned.1.call-start = ((), (), s32[]{:S(2)}) async-start(), calls=%async_computation.14 | async-start | bytes 9437184 | tf_op jit(solution)/shard_map/all_gather | solution.py:94
  109.0 294.9 %all-gather.23.cloned.1.call-start = ((), (), s32[]{:S(2)}) async-start(), calls=%async_computation.15 | async-start | bytes 28311552 | tf_op jit(solution)/shard_map/all_gather | solution.py:98
  114.0 417.7 %all-gather.25.cloned.1.call-start = ((), (), s32[]{:S(2)}) async-start(), calls=%async_computation.16 | async-start | bytes 28311552 | tf_op jit(solution)/shard_map/all_gather | solution.py:99
  119.0 540.6 %all-gather.27.cloned.1.call-start = ((), (), s32[]{:S(2)}) async-start(), calls=%async_computation.17 | async-start | bytes 28311552 | tf_op jit(solution)/shard_map/all_gather | solution.py:100
  124.0 874.9 %reduce-scatter.11.cloned.1.call-start = ((), (), s32[]{:S(2)}) async-start(), calls=%async_computation.18 | async-start | bytes 5242880 | tf_op jit(solution)/shard_map/reduce_scatter | solution.py:264
  142.5 200.2 %copy-start.33 = (f32[512,16]{0,1:T(8,128)}, f32[512,16]{0,1:T(8,128)S(1)}, u32[]{:S(2)}) copy-start(f32[512,16]{0,1:T(8,128)S(1)} %fusion.115) | copy-start | bytes 98308
  424.9 234.7 %copy-start.49 = (f32[512]{0:T(512)S(1)}, f32[512]{0:T(512)}, u32[]{:S(2)}) copy-start(f32[512]{0:T(512)} %get-tuple-element.297) | copy-start | bytes 6148
  954.3 91.9 %reduce-scatter.13.cloned.1.call-start = ((), (), s32[]{:S(2)}) async-start(), calls=%async_computation.19 | async-start | bytes 5242880 | tf_op jit(solution)/shard_map/reduce_scatter | solution.py:267
  955.0 173.0 %reduce-scatter.15.cloned.1.call-start = ((), (), s32[]{:S(2)}) async-start(), calls=%async_computation.20 | async-start | bytes 9437184 | tf_op jit(solution)/shard_map/reduce_scatter | solution.py:306
  971.9 224.1 %reduce-scatter.23.cloned.1.call-start = ((), (), s32[]{:S(2)}) async-start(), calls=%async_computation.24 | async-start | bytes 9437184 | tf_op jit(solution)/shard_map/reduce_scatter | solution.py:324
  983.3 267.3 %reduce-scatter.17.cloned.1.call-start = ((), (), s32[]{:S(2)}) async-start(), calls=%async_computation.21 | async-start | bytes 4718592 | tf_op jit(solution)/shard_map/reduce_scatter | solution.py:309
  1009.7 295.8 %reduce-scatter.19.cloned.1.call-start = ((), (), s32[]{:S(2)}) async-start(), calls=%async_computation.22 | async-start | bytes 4718592 | tf_op jit(solution)/shard_map/reduce_scatter | solution.py:312
  1052.0 413.9 %reduce-scatter.25.cloned.1.call-start = ((), (), s32[]{:S(2)}) async-start(), calls=%async_computation.25 | async-start | bytes 28311552 | tf_op jit(solution)/shard_map/reduce_scatter | solution.py:201
  1072.8 553.5 %reduce-scatter.27.cloned.1.call-start = ((), (), s32[]{:S(2)}) async-start(), calls=%async_computation.26 | async-start | bytes 28311552 | tf_op jit(solution)/shard_map/reduce_scatter | solution.py:204
  1094.7 691.9 %reduce-scatter.29.cloned.1.call-start = ((), (), s32[]{:S(2)}) async-start(), calls=%async_computation.27 | async-start | bytes 28311552 | tf_op jit(solution)/shard_map/reduce_scatter | solution.py:207
  1116.2 728.0 %reduce-scatter.21.cloned.1.call-start = ((), (), s32[]{:S(2)}) async-start(), calls=%async_computation.23 | async-start | bytes 73728 | tf_op jit(solution)/shard_map/reduce_scatter | solution.py:321
  1127.8 1128.2 %all-reduce.12.cloned.1.call-start = ((), (), s32[]{:S(2)}) async-start(), calls=%async_computation.29 | async-start | bytes 25165824 | tf_op jit(solution)/shard_map/psum | solution.py:330
  (81 other events, 800.2 us)
Sparse Core Ops, SparseCore 0:
  10.5 39.4 all-gather.12
  52.4 36.9 all-gather.14
  91.5 34.4 all-gather.28
  128.0 34.5 all-gather.16
  164.9 54.3 all-gather.18
  221.6 54.3 all-gather.20
  278.5 125.3 all-gather.22
  406.3 125.3 all-gather.24
  534.2 125.3 all-gather.26
  954.4 44.4 reduce-scatter.10
  1001.6 44.5 reduce-scatter.12
  1049.5 71.2 reduce-scatter.14
  1124.7 71.2 reduce-scatter.22
  1199.2 51.3 reduce-scatter.16
  1254.1 51.3 reduce-scatter.18
  1309.0 156.8 reduce-scatter.24
  1469.3 156.8 reduce-scatter.26
  1629.7 156.8 reduce-scatter.28
  1790.2 31.4 reduce-scatter.20
  1825.3 430.6 all-reduce.11
where the time goes:
time: 2290 us; the launch traced here: 2280 us
  waiting for transfers between devices  1460 us (64%)
  matrix products  492 us (21%)
  other arithmetic  147 us (6%)
  local copies, waits for them, and re-layouts  83.6 us (4%)
  blocking collectives  79.9 us (3%)
    psum x1, waiting for transfers between devices, body(): lax.psum(attn_shares[1].astype(jnp.bfloat16), 'rep').astype(jnp.float32)  383 us
    reduce_scatter x1, waiting for transfers between devices, body(): lax.psum_scatter(grad_gateff_term.astype(jnp.bfloat16), ('dp', 'ctx'), sc...  160 us
    reduce_scatter x1, waiting for transfers between devices, body(): lax.psum_scatter(grad_down_term.astype(jnp.bfloat16), ('dp', 'ctx'), scat...  160 us
    reduce_scatter x1, waiting for transfers between devices, body(): lax.psum_scatter(grad_up_term.astype(jnp.bfloat16), ('dp', 'ctx'), scatte...  160 us
    all_gather x1, waiting for transfers between devices, body(): lax.all_gather(shard_wd, ('dp', 'ctx'), axis=0, tiled=True)  107 us
    all_gather x1, waiting for transfers between devices, body(): lax.all_gather(shard_wu, ('dp', 'ctx'), axis=0, tiled=True)  107 us
    dot_general x8, matrix products, through_rows(): lax.dot_general(left, right, (((1,), (1,)), ((), ())), preferred_element_...  103 us
    dot_general x8, matrix products, outer_sum(): lax.dot_general(left, right, (((0,), (0,)), ((), ())), preferred_element_...  93.4 us
  transfers between devices with their start and end apart: 20, of which 16 were waited for; matrix products, arithmetic and copies ran while one was open for 17% of the time, Pallas kernels for 0%

commit v1 on v0

v1 whole, which is shorter than its diff:
```python
import jax
import jax.numpy as jnp
from jax import lax
from jax.experimental import pallas as pl
from jax.experimental.pallas import tpu as pltpu
from jax.sharding import PartitionSpec as P

QUERY_HEADS = 16
KEY_VALUE_HEADS = 8
HEAD_SIZE = 128
GROUP = QUERY_HEADS // KEY_VALUE_HEADS
DOCS = 32
BLOCK = 256

epsilon = 1e-06
masked_score = -1e30
scale = HEAD_SIZE ** (-0.5)
half = jnp.bfloat16
f32 = jnp.float32


def inverse_root(value):
    return lax.rsqrt(jnp.mean(value * value, axis=-1, keepdims=True) + epsilon)


def norm_pullback(grad_in, normed_rows, inverse, gain):
    scaled = grad_in * gain
    return inverse * (scaled - normed_rows * jnp.mean(normed_rows * scaled, axis=-1, keepdims=True))


def matrix_product(left, right):
    return jnp.dot(left, right, preferred_element_type=f32)


def outer_sum(left, right):
    return lax.dot_general(left, right, (((0,), (0,)), ((), ())), preferred_element_type=f32)


def through_rows(left, right):
    return lax.dot_general(left, right, (((1,), (1,)), ((), ())), preferred_element_type=f32)


def place_of(block, where_ref, per):
    return ((block // per) ^ where_ref[0]) * per + block % per


def stack_heads(ref, group):
    first = group * GROUP * HEAD_SIZE
    return jnp.concatenate(
        [ref[:, first + h * HEAD_SIZE : first + (h + 1) * HEAD_SIZE] for h in range(GROUP)], axis=0
    )


def stack_columns(ref, first):
    return jnp.concatenate([ref[:, first + h : first + h + 1] for h in range(GROUP)], axis=0)


def allowed_block(start_ref, block, keys):
    rows = lax.broadcasted_iota(jnp.int32, (GROUP * BLOCK, BLOCK), 0)
    spot_query = block * BLOCK + jnp.where(rows >= BLOCK, rows - BLOCK, rows)
    spot_key = keys * BLOCK + lax.broadcasted_iota(jnp.int32, (GROUP * BLOCK, BLOCK), 1)
    start = jnp.concatenate([start_ref[...]] * GROUP, axis=0)
    return (spot_key >= start) & (spot_key <= spot_query)


def attention_forward(where_ref, low_ref, qkva, start, gain_q, gain_k, gated, mixed, log_norm, keys, values, scores, *, groups):
    block = pl.program_id(0)
    q_width = groups * GROUP * HEAD_SIZE
    kv_width = groups * HEAD_SIZE
    here = pl.ds(pl.multiple_of(block * BLOCK, BLOCK), BLOCK)
    for g in range(groups):
        at = slice(g * HEAD_SIZE, (g + 1) * HEAD_SIZE)
        k = qkva[:, q_width + g * HEAD_SIZE : q_width + (g + 1) * HEAD_SIZE]
        keys[here, at] = (k * inverse_root(k) * gain_k[...]).astype(half)
        v = qkva[:, q_width + kv_width + g * HEAD_SIZE : q_width + kv_width + (g + 1) * HEAD_SIZE]
        values[here, at] = v.astype(half)
    low = low_ref[block]
    lane = lax.broadcasted_iota(jnp.int32, (BLOCK, HEAD_SIZE), 1)
    norms = jnp.zeros((BLOCK, HEAD_SIZE), f32)
    for g in range(groups):
        at = slice(g * HEAD_SIZE, (g + 1) * HEAD_SIZE)
        q = stack_heads(qkva, g)
        qn = (q * inverse_root(q) * gain_q[...]).astype(half)

        def score_step(j, peak):
            span = pl.ds(pl.multiple_of(j * BLOCK, BLOCK), BLOCK)
            s = through_rows(qn, keys[span, at]) * scale
            s = jnp.where(allowed_block(start, block, j), s, masked_score)
            scores[:, span] = s
            return jnp.maximum(peak, jnp.max(s, axis=-1, keepdims=True))

        peak = lax.fori_loop(low, block + 1, score_step, jnp.full((GROUP * BLOCK, 1), masked_score, f32))

        def exp_step(j, total):
            span = pl.ds(pl.multiple_of(j * BLOCK, BLOCK), BLOCK)
            e = jnp.exp(scores[:, span] - peak)
            scores[:, span] = e
            return total + jnp.sum(e, axis=-1, keepdims=True)

        total = lax.fori_loop(low, block + 1, exp_step, jnp.zeros((GROUP * BLOCK, 1), f32))

        def mix_step(j, mix):
            span = pl.ds(pl.multiple_of(j * BLOCK, BLOCK), BLOCK)
            p = (scores[:, span] / total).astype(half)
            return mix + matrix_product(p, values[span, at])

        mix = lax.fori_loop(low, block + 1, mix_step, jnp.zeros((GROUP * BLOCK, HEAD_SIZE), f32))
        lse = peak + jnp.log(total)
        for h in range(GROUP):
            head = g * GROUP + h
            to = slice(head * HEAD_SIZE, (head + 1) * HEAD_SIZE)
            o = mix[h * BLOCK : (h + 1) * BLOCK]
            gate = jax.nn.sigmoid(qkva[:, q_width + 2 * kv_width + head : q_width + 2 * kv_width + head + 1])
            mixed[:, to] = o
            gated[:, to] = (o * gate).astype(half)
            norms = jnp.where(lane == head, lse[h * BLOCK : (h + 1) * BLOCK], norms)
    log_norm[...] = norms


def attention_backward(
    where_ref, low_ref, qkva, start, gain_q, gain_k, mixed, log_norm, grad_gated,
    grad_qkva, grad_gains,
    keys, values, raw_keys, grad_keys, grad_values, probs, grad_probs, *, groups, per,
):
    block = pl.program_id(0)
    blocks = pl.num_programs(0)
    q_width = groups * GROUP * HEAD_SIZE
    kv_width = groups * HEAD_SIZE
    here = pl.ds(pl.multiple_of(block * BLOCK, BLOCK), BLOCK)
    out_rows = pl.ds(pl.multiple_of(place_of(block, where_ref, per) * BLOCK, BLOCK), BLOCK)

    @pl.when(block == 0)
    def _():
        grad_gains[...] = jnp.zeros_like(grad_gains)

    for g in range(groups):
        at = slice(g * HEAD_SIZE, (g + 1) * HEAD_SIZE)
        k = qkva[:, q_width + g * HEAD_SIZE : q_width + (g + 1) * HEAD_SIZE]
        raw_keys[here, at] = k
        keys[here, at] = (k * inverse_root(k) * gain_k[...]).astype(half)
        v = qkva[:, q_width + kv_width + g * HEAD_SIZE : q_width + kv_width + (g + 1) * HEAD_SIZE]
        values[here, at] = v.astype(half)
    grad_keys[here, :] = jnp.zeros((BLOCK, kv_width), f32)
    grad_values[here, :] = jnp.zeros((BLOCK, kv_width), f32)
    low = low_ref[block]
    lane = lax.broadcasted_iota(jnp.int32, (BLOCK, HEAD_SIZE), 1)
    grad_logits = jnp.zeros((BLOCK, HEAD_SIZE), f32)
    for g in range(groups):
        at = slice(g * HEAD_SIZE, (g + 1) * HEAD_SIZE)
        q = stack_heads(qkva, g)
        rq = inverse_root(q)
        nq = q * rq
        qn = (nq * gain_q[...]).astype(half)
        lse = stack_columns(log_norm, g * GROUP)
        gate = jax.nn.sigmoid(stack_columns(qkva, q_width + 2 * kv_width + g * GROUP))
        upstream = stack_heads(grad_gated, g).astype(f32)
        o = stack_heads(mixed, g)
        da = jnp.sum(upstream * o, axis=-1, keepdims=True) * gate * (1.0 - gate)
        do = (upstream * gate).astype(half)
        for h in range(GROUP):
            grad_logits = jnp.where(lane == g * GROUP + h, da[h * BLOCK : (h + 1) * BLOCK], grad_logits)

        def prob_step(j, delta):
            span = pl.ds(pl.multiple_of(j * BLOCK, BLOCK), BLOCK)
            s = through_rows(qn, keys[span, at]) * scale
            p = jnp.where(allowed_block(start, block, j), jnp.exp(s - lse), 0.0)
            dp = through_rows(do, values[span, at])
            probs[:, span] = p
            grad_probs[:, span] = dp
            grad_values[span, at] += outer_sum(p.astype(half), do)
            return delta + jnp.sum(p * dp, axis=-1, keepdims=True)

        delta = lax.fori_loop(low, block + 1, prob_step, jnp.zeros((GROUP * BLOCK, 1), f32))

        def score_step(j, dq):
            span = pl.ds(pl.multiple_of(j * BLOCK, BLOCK), BLOCK)
            ds = (probs[:, span] * (grad_probs[:, span] - delta)).astype(half)
            grad_keys[span, at] += outer_sum(ds, qn)
            return dq + matrix_product(ds, keys[span, at])

        dqn = lax.fori_loop(low, block + 1, score_step, jnp.zeros((GROUP * BLOCK, HEAD_SIZE), f32)) * scale
        grad_gains[0:1, :] += jnp.sum(dqn * nq, axis=0, keepdims=True)
        dq = norm_pullback(dqn, nq, rq, gain_q[...]).astype(half)
        for h in range(GROUP):
            head = g * GROUP + h
            grad_qkva[out_rows, head * HEAD_SIZE : (head + 1) * HEAD_SIZE] = dq[h * BLOCK : (h + 1) * BLOCK]
    grad_qkva[out_rows, q_width + 2 * kv_width :] = grad_logits.astype(half)

    @pl.when(block == blocks - 1)
    def _():
        def finish(j, carry):
            span = pl.ds(pl.multiple_of(j * BLOCK, BLOCK), BLOCK)
            rows = pl.ds(pl.multiple_of(place_of(j, where_ref, per) * BLOCK, BLOCK), BLOCK)
            for g in range(groups):
                at = slice(g * HEAD_SIZE, (g + 1) * HEAD_SIZE)
                k = raw_keys[span, at]
                rk = inverse_root(k)
                nk = k * rk
                dkn = grad_keys[span, at] * scale
                grad_gains[1:2, :] += jnp.sum(dkn * nk, axis=0, keepdims=True)
                dk = norm_pullback(dkn, nk, rk, gain_k[...]).astype(half)
                grad_qkva[rows, q_width + g * HEAD_SIZE : q_width + (g + 1) * HEAD_SIZE] = dk
                grad_qkva[rows, q_width + kv_width + g * HEAD_SIZE : q_width + kv_width + (g + 1) * HEAD_SIZE] = (
                    grad_values[span, at].astype(half)
                )
            return carry

        lax.fori_loop(0, blocks, finish, 0)


def run_attention_forward(qkva, start, low, where, gain_q, gain_k, per):
    length, width = qkva.shape
    groups = (width - HEAD_SIZE) // ((GROUP + 2) * HEAD_SIZE)
    q_width = groups * GROUP * HEAD_SIZE
    kv_width = groups * HEAD_SIZE

    def rows(i, where_ref, low_ref):
        return (place_of(i, where_ref, per), 0)

    def whole(i, where_ref, low_ref):
        return (0, 0)

    def body(*refs):
        attention_forward(*refs, groups=groups)

    pairs = length * length // 2
    return pl.pallas_call(
        body,
        grid_spec=pltpu.PrefetchScalarGridSpec(
            num_scalar_prefetch=2,
            grid=(length // BLOCK,),
            in_specs=[
                pl.BlockSpec((BLOCK, width), rows),
                pl.BlockSpec((BLOCK, 1), lambda i, where_ref, low_ref: (i, 0)),
                pl.BlockSpec((1, HEAD_SIZE), whole),
                pl.BlockSpec((1, HEAD_SIZE), whole),
            ],
            out_specs=[
                pl.BlockSpec((BLOCK, q_width), rows),
                pl.BlockSpec((BLOCK, q_width), rows),
                pl.BlockSpec((BLOCK, HEAD_SIZE), rows),
            ],
            scratch_shapes=[
                pltpu.VMEM((length, kv_width), half),
                pltpu.VMEM((length, kv_width), half),
                pltpu.VMEM((GROUP * BLOCK, length), f32),
            ],
        ),
        out_shape=(
            jax.ShapeDtypeStruct((length, q_width), half),
            jax.ShapeDtypeStruct((length, q_width), f32),
            jax.ShapeDtypeStruct((length, HEAD_SIZE), f32),
        ),
        cost_estimate=pl.CostEstimate(
            flops=pairs * q_width * 2, bytes_accessed=length * (width + q_width) * 4, transcendentals=pairs * groups
        ),
        name="attention_forward",
    )(where, low, qkva, start, gain_q, gain_k)


def run_attention_backward(qkva, start, low, where, gain_q, gain_k, mixed, log_norm, grad_gated, per):
    length, width = qkva.shape
    groups = (width - HEAD_SIZE) // ((GROUP + 2) * HEAD_SIZE)
    q_width = groups * GROUP * HEAD_SIZE
    kv_width = groups * HEAD_SIZE

    def rows(i, where_ref, low_ref):
        return (place_of(i, where_ref, per), 0)

    def whole(i, where_ref, low_ref):
        return (0, 0)

    def body(*refs):
        attention_backward(*refs, groups=groups, per=per)

    pairs = length * length // 2
    return pl.pallas_call(
        body,
        grid_spec=pltpu.PrefetchScalarGridSpec(
            num_scalar_prefetch=2,
            grid=(length // BLOCK,),
            in_specs=[
                pl.BlockSpec((BLOCK, width), rows),
                pl.BlockSpec((BLOCK, 1), lambda i, where_ref, low_ref: (i, 0)),
                pl.BlockSpec((1, HEAD_SIZE), whole),
                pl.BlockSpec((1, HEAD_SIZE), whole),
                pl.BlockSpec((BLOCK, q_width), rows),
                pl.BlockSpec((BLOCK, HEAD_SIZE), rows),
                pl.BlockSpec((BLOCK, q_width), rows),
            ],
            out_specs=[
                pl.BlockSpec((length, width), whole),
                pl.BlockSpec((8, HEAD_SIZE), whole),
            ],
            scratch_shapes=[
                pltpu.VMEM((length, kv_width), half),
                pltpu.VMEM((length, kv_width), half),
                pltpu.VMEM((length, kv_width), f32),
                pltpu.VMEM((length, kv_width), f32),
                pltpu.VMEM((length, kv_width), f32),
                pltpu.VMEM((GROUP * BLOCK, length), f32),
                pltpu.VMEM((GROUP * BLOCK, length), f32),
            ],
        ),
        out_shape=(
            jax.ShapeDtypeStruct((length, width), half),
            jax.ShapeDtypeStruct((8, HEAD_SIZE), f32),
        ),
        cost_estimate=pl.CostEstimate(
            flops=pairs * q_width * 5, bytes_accessed=length * (width + q_width) * 6, transcendentals=pairs * groups
        ),
        name="attention_backward",
    )(where, low, qkva, start, gain_q, gain_k, mixed, log_norm, grad_gated)


def after(x, *others):
    return lax.optimization_barrier((x,) + others)[0]


def build(rep_size, dp_size, ctx_size):
    R, D, C = rep_size, dp_size, ctx_size
    pair = D == 2
    spread = D if KEY_VALUE_HEADS % (D * C) == 0 else 1
    groups = KEY_VALUE_HEADS // C
    q_width = groups * GROUP * HEAD_SIZE
    kv_width = groups * HEAD_SIZE

    def hop(x, k):
        if k == 0:
            return x
        return lax.ppermute(x, "ctx", [(i, i ^ k) for i in range(C)])

    def other_dp(x):
        return lax.ppermute(x, "dp", [(i, 1 - i) for i in range(2)])

    def gather_blocks(x):
        far = hop(x, 2)
        return [x, hop(x, 1), far, hop(far, 1)]

    def scatter_blocks(near, far):
        rows = near.shape[0] // 2
        cross = hop(far[rows:].astype(half), 1)
        across = hop((far[:rows] + cross.astype(f32)).astype(half), 2)
        beside = hop(near[rows:].astype(half), 1)
        return near[:rows] + beside.astype(f32) + across.astype(f32)

    def total_over(x):
        for k in (1, 2):
            x = x + hop(x, k)
        x = x + other_dp(x) if pair else lax.psum(x, "dp")
        if R == 4:
            for k in (1, 2):
                x = x + lax.ppermute(x, "rep", [(i, i ^ k) for i in range(R)])
            return x
        return lax.psum(x, "rep")

    def body(
        hidden_in, segments, cotangent, attn_gain, w_query, key_projection, value_projection,
        q_gain, k_gain, w_gate, w_out, mlp_gain, w_gate_ff, w_up, w_down,
    ):
        sequences, rows, model = hidden_in.shape
        assert sequences == 1 and C == 4
        length = rows * C
        dp = lax.axis_index("dp")
        ctx = lax.axis_index("ctx")
        part = attn_gain.shape[0]
        hp = q_gain.shape[0]
        units = w_down.shape[0]

        def at_row(x, first, count):
            return lax.dynamic_slice_in_dim(x, first, count, axis=0)

        def at_column(x, first, count):
            return lax.dynamic_slice_in_dim(x, first, count, axis=1)

        def put_row(buffer, x, first):
            return lax.dynamic_update_slice_in_dim(buffer, x, first, axis=0)

        def put_column(buffer, x, first):
            return lax.dynamic_update_slice_in_dim(buffer, x, first, axis=1)

        def first_mine(x):
            m = x.shape[0] // 2
            return jnp.where(dp == 0, x, jnp.concatenate([x[m:], x[:m]], axis=0))

        def head_columns(w, per_head, c):
            w = w.reshape(part, spread, C, -1)
            return lax.dynamic_index_in_dim(w, c, axis=2, keepdims=False).reshape(part, groups * per_head)

        def unit_columns(w, c):
            w = w.reshape(part, D, C, units)
            return lax.dynamic_index_in_dim(w, c, axis=2, keepdims=False).reshape(part, D * units)

        def gather_rows(blocks):
            width = blocks[0].shape[1]
            got = [hop(b, k) for k, b in enumerate(blocks)]
            if not pair:
                mine = jnp.zeros((C * part, width), half)
                for k in range(C):
                    mine = put_row(mine, got[k], (ctx ^ k) * part)
                return lax.all_gather(mine, "dp", axis=0, tiled=True), got
            whole = jnp.zeros((D * C * part, width), half)
            away = [other_dp(b) for b in got]
            for k in range(C):
                whole = put_row(whole, got[k], (dp * C + (ctx ^ k)) * part)
                whole = put_row(whole, away[k], ((1 - dp) * C + (ctx ^ k)) * part)
            return whole, got

        def split_product(left_near, left_far, right_near, right_far):
            count = left_near.shape[1] // D
            if not pair:
                grad = outer_sum(left_near, right_near) + outer_sum(left_far, right_far)
                return lax.psum_scatter(grad.astype(half), "dp", scatter_dimension=0, tiled=True)
            other, own = (1 - dp) * count, dp * count
            away = outer_sum(at_column(left_near, other, count), right_near) + outer_sum(
                at_column(left_far, other, count), right_far
            )
            away = other_dp(away.astype(half))
            mine = outer_sum(at_column(left_near, own, count), right_near) + outer_sum(
                at_column(left_far, own, count), right_far
            )
            return (mine + away.astype(f32)).astype(half)

        def return_rows(total):
            return [hop(at_row(total, (ctx ^ k) * part, part), k) for k in range(C)]

        small = jnp.concatenate([attn_gain, mlp_gain, q_gain, k_gain, segments[0].astype(f32)]).astype(half)
        small = lax.all_gather(small, ("dp", "ctx"), axis=0, tiled=False)
        ready = small
        small = small.astype(f32)
        gain_a = small[:, :part].reshape(1, -1)
        gain_m = small[:, part : 2 * part].reshape(1, -1)
        gain_q = small[:, 2 * part : 2 * part + hp].reshape(1, -1)
        gain_k = small[:, 2 * part + hp : 2 * part + 2 * hp].reshape(1, -1)
        seq_segments = at_row(small[:, 2 * part + 2 * hp :], dp * C, C).reshape(-1)

        doc = lax.broadcasted_iota(jnp.int32, (DOCS, 1), 0).astype(f32)
        live = seq_segments >= 0
        before = jnp.sum(jnp.where(live[None, :] & (seq_segments[None, :] < doc), 1.0, 0.0), axis=1)
        start_of = jnp.sum(jnp.where(seq_segments[:, None] == doc[:, 0][None, :], before[None, :], 0.0), axis=1)
        spot = lax.broadcasted_iota(jnp.int32, (length,), 0)
        start = jnp.where(live, start_of.astype(jnp.int32), spot)
        low = start[::BLOCK] // BLOCK
        start = start[:, None]
        where = ctx.reshape(1).astype(jnp.int32)

        pad = HEAD_SIZE - groups * GROUP
        attn_blocks = [
            jnp.concatenate(
                [
                    head_columns(w_query, GROUP * HEAD_SIZE, ctx ^ k),
                    head_columns(key_projection, HEAD_SIZE, ctx ^ k),
                    head_columns(value_projection, HEAD_SIZE, ctx ^ k),
                    jnp.pad(head_columns(w_gate, GROUP, ctx ^ k), ((0, 0), (0, pad))),
                ],
                axis=1,
            ).astype(half)
            for k in range(C)
        ]
        w_qkva, attn_got = gather_rows([after(b, ready) for b in attn_blocks])
        x_own = hidden_in[0]
        x_blocks = gather_blocks(after(x_own, ready))
        x_all = jnp.concatenate(x_blocks, axis=0).astype(f32)
        hn = (x_all * inverse_root(x_all) * gain_a).astype(half)

        w_gate_ff_all, gate_got = gather_rows(
            [after(unit_columns(w_gate_ff, ctx ^ k).astype(half), x_blocks[2]) for k in range(C)]
        )
        w_out_half = after(w_out.astype(half), ready)
        if spread == D and pair:
            w_out_mine = first_mine(jnp.concatenate([w_out_half, other_dp(w_out_half)], axis=0))
            w_out_all = jnp.concatenate(gather_blocks(after(w_out_mine, hn)), axis=0)
        else:
            w_out_full = lax.all_gather(w_out_half, ("dp", "ctx"), axis=0, tiled=True)
            span = w_out_full.shape[0] // C
            w_out_all = jnp.concatenate([at_row(w_out_full, (ctx ^ k) * span, span) for k in range(C)], axis=0)

        qkva = matrix_product(hn, w_qkva)
        w_down_half = after(w_down.astype(half), qkva)
        if pair:
            w_down_all = first_mine(jnp.concatenate([w_down_half, other_dp(w_down_half)], axis=0))
        else:
            w_down_all = lax.all_gather(w_down_half, "dp", axis=0, tiled=True)
        gated, mixed, log_norm = run_attention_forward(
            qkva, start, low, where, gain_q, gain_k, rows // BLOCK
        )
        w_up_all, up_got = gather_rows([after(unit_columns(w_up, ctx ^ k).astype(half), gated) for k in range(C)])
        gated_own = jnp.concatenate(
            [hop(gated[k * rows : (k + 1) * rows], k) for k in range(C)], axis=1
        )
        x_f = x_own.astype(f32)
        x1 = x_f + matrix_product(gated_own, w_out_all)
        inverse_m = inverse_root(x1)
        nm = x1 * inverse_m
        hm_own = (nm * gain_m).astype(half)
        hm = gather_blocks(hm_own)
        hm = (jnp.concatenate(hm[:2], axis=0), jnp.concatenate(hm[2:], axis=0))

        valid = (segments.reshape(rows, 1) >= 0).astype(f32)
        dy_own = cotangent[0].astype(f32) * valid
        dy = gather_blocks(after(dy_own.astype(half), hm_own))
        dy = (jnp.concatenate(dy[:2], axis=0), jnp.concatenate(dy[2:], axis=0))

        hidden, grad_gate_half, grad_up_half = [], [], []
        for rows_m, rows_dy in zip(hm, dy):
            gate_ff = matrix_product(rows_m, w_gate_ff_all)
            up_ff = matrix_product(rows_m, w_up_all)
            grad_hidden = through_rows(rows_dy, w_down_all)
            sig = jax.nn.sigmoid(gate_ff)
            hidden.append((gate_ff * sig * up_ff).astype(half))
            grad_gate_half.append((grad_hidden * up_ff * sig * (1.0 + gate_ff * (1.0 - sig))).astype(half))
            grad_up_half.append((grad_hidden * gate_ff * sig).astype(half))
        dhm_parts = [
            through_rows(a, w_gate_ff_all) + through_rows(b, w_up_all)
            for a, b in zip(grad_gate_half, grad_up_half)
        ]
        dhm = scatter_blocks(*dhm_parts)
        grad_gm = jnp.sum(dhm * nm, axis=0)
        dx1 = dy_own + norm_pullback(dhm, nm, inverse_m, gain_m)
        dx1_half = dx1.astype(half)

        grad_down = split_product(hidden[0], hidden[1], dy[0], dy[1])
        grad_down = lax.psum(grad_down, "rep")
        grad_gate_ff = split_product(hm[0], hm[1], grad_gate_half[0], grad_gate_half[1])
        grad_gate_ff = lax.psum(after(grad_gate_ff, grad_down), "rep")
        grad_up = split_product(hm[0], hm[1], grad_up_half[0], grad_up_half[1])
        grad_up = lax.psum(after(grad_up, grad_gate_ff), "rep")

        y = scatter_blocks(*[matrix_product(h, w_down_all) for h in hidden])
        layer_out = (x1 + y).astype(half)[None]

        grad_gated_own = through_rows(dx1_half, w_out_all).astype(half)
        grad_gated = jnp.concatenate(
            [hop(grad_gated_own[:, k * q_width : (k + 1) * q_width], k) for k in range(C)], axis=0
        )
        dx1_blocks = gather_blocks(after(dx1_half, grad_gated_own))
        dx1_near, dx1_far = jnp.concatenate(dx1_blocks[:2], axis=0), jnp.concatenate(dx1_blocks[2:], axis=0)
        gated_near, gated_far = gated[: 2 * rows], gated[2 * rows :]
        if spread == D and pair:
            grad_out = split_product(gated_near, gated_far, dx1_near, dx1_far)
        else:
            grad_out = outer_sum(gated_near, dx1_near) + outer_sum(gated_far, dx1_far)
            grad_out = put_row(jnp.zeros((model, model), half), grad_out.astype(half), ctx * grad_out.shape[0])
            grad_out = lax.psum_scatter(grad_out, ("dp", "ctx"), scatter_dimension=0, tiled=True)
        grad_out = lax.psum(after(grad_out, grad_up), "rep")

        grad_qkva, grad_gains = run_attention_backward(
            qkva, start, low, where, gain_q, gain_k, mixed, log_norm, grad_gated, rows // BLOCK
        )
        grad_attn = split_product(hn[: 2 * rows], hn[2 * rows :], grad_qkva[: 2 * rows], grad_qkva[2 * rows :])
        grad_attn = lax.psum(after(grad_attn, grad_out), "rep")
        dhn = scatter_blocks(
            through_rows(grad_qkva[: 2 * rows], w_qkva), through_rows(grad_qkva[2 * rows :], w_qkva)
        )
        inverse_a = inverse_root(x_f)
        na = x_f * inverse_a
        grad_ga = jnp.sum(dhn * na, axis=0)
        input_grad = (dx1 + norm_pullback(dhn, na, inverse_a, gain_a)).astype(half)[None]

        def unit_grad(total):
            out = jnp.zeros((part, D * C * units), f32)
            for k, b in enumerate(return_rows(total)):
                for d in range(D):
                    piece = b[:, d * units : (d + 1) * units].astype(f32)
                    out = put_column(out, piece, (d * C + (ctx ^ k)) * units)
            return out

        attn_back = return_rows(grad_attn)

        def head_grad(first, width):
            per = width // spread
            out = jnp.zeros((part, C * width), f32)
            for k, b in enumerate(attn_back):
                for d in range(spread):
                    piece = b[:, first + d * per : first + (d + 1) * per].astype(f32)
                    out = put_column(out, piece, (d * C + (ctx ^ k)) * per)
            return out

        gains = total_over(jnp.concatenate([grad_ga, grad_gm, grad_gains[0], grad_gains[1]]).reshape(-1, HEAD_SIZE))
        gains = gains.reshape(-1)
        at = dp * C + ctx
        return (
            layer_out,
            input_grad,
            at_row(gains, at * part, part),
            head_grad(0, q_width),
            head_grad(q_width, kv_width),
            head_grad(q_width + kv_width, kv_width),
            at_row(gains, 2 * model + at * hp, hp),
            at_row(gains, 2 * model + HEAD_SIZE + at * hp, hp),
            head_grad(q_width + 2 * kv_width, groups * GROUP),
            grad_out.astype(f32),
            at_row(gains, model + at * part, part),
            unit_grad(grad_gate_ff),
            unit_grad(grad_up),
            grad_down.astype(f32),
        )

    return body


def solution(mesh):
    tokens = P(("rep", "dp"), "ctx", None)
    vector = P(("dp", "ctx"))
    matrix = P(("dp", "ctx"), None)
    weights = (vector, matrix, matrix, matrix, vector, vector, matrix, matrix, vector, matrix, matrix, matrix)
    return jax.shard_map(
        build(mesh.shape["rep"], mesh.shape["dp"], mesh.shape["ctx"]),
        mesh=mesh,
        in_specs=(tokens, P(("rep", "dp"), "ctx"), tokens) + weights,
        out_specs=(tokens, tokens) + weights,
        check_vma=False,
    )
```

time: 2290 us -> 1450 us (0.63)
  waiting for transfers between devices: 1460 us -> 682 us
  matrix products: 492 us -> 299 us
  Pallas kernels: 0 us -> 93.8 us
  blocking collectives: 79.9 us -> 10.6 us
  starting transfers between devices: 1.83 us -> 51.9 us
  local copies, waits for them, and re-layouts: 83.6 us -> 132 us
    reduce_scatter x10 -> x0, waiting for transfers between devices: 710 us -> none  [the longest x1 160 us: body(): lax.psum_scatter(grad_gateff_term.astype(jnp.bfloat16), ('dp', 'ctx'), sc...]
    ppermute x0 -> x72, waiting for transfers between devices: none -> 429 us  [the longest x20 341 us: other_dp(): return lax.ppermute(x, 'dp', [(i, 1 - i) for i in range(2)])]
    all_gather x9 -> x0, waiting for transfers between devices: 365 us -> none  [the longest x1 107 us: body(): lax.all_gather(shard_wd, ('dp', 'ctx'), axis=0, tiled=True)]
    dot_general x64 -> x8, matrix products: 295 us -> 94.5 us  [matrix_product(): return jnp.dot(left, right, preferred_element_type=f32)]
    psum x1 -> x5, waiting for transfers between devices: 383 us -> 254 us  [the longest x1 83.2 us: body(): grad_up = lax.psum(after(grad_up, grad_gate_ff), 'rep')]
    pallas_call x0 -> x2, Pallas kernels: none -> 93.8 us  [the longest x1 56.1 us: run_attention_backward(): pl.pallas_call(body, grid_spec=pltpu.PrefetchScalarGridSpec(num_scalar_pr...]
    ppermute x0 -> x72, starting transfers between devices: none -> 51.7 us  [the longest x50 29.4 us: hop(): return lax.ppermute(x, 'ctx', [(i, i ^ k) for i in range(C)])]
    dynamic_update_slice x8 -> x44, other arithmetic: 4.78 us -> 47.2 us  [put_column(): return lax.dynamic_update_slice_in_dim(buffer, x, first, axis=1)]
  transfers between devices with their start and end apart: 20 -> 77, of which waited for: 16 -> 30; matrix products, arithmetic and copies ran while one was open for 17% -> 36% of each run, Pallas kernels for 0% -> 6%
where the time goes in v1:
time: 1450 us; the launch traced here: 1440 us
  waiting for transfers between devices  682 us (47%)
  matrix products  299 us (21%)
  other arithmetic  159 us (11%)
  local copies, waits for them, and re-layouts  132 us (9%)
  Pallas kernels  93.8 us (6%)
  starting transfers between devices  51.9 us (4%)
  between operations  15.8 us (1%)
    ppermute x20, waiting for transfers between devices, other_dp(): return lax.ppermute(x, 'dp', [(i, 1 - i) for i in range(2)])  341 us
    dot_general x20, matrix products, outer_sum(): lax.dot_general(left, right, (((0,), (0,)), ((), ())), preferred_element_...  114 us
    dot_general x8, matrix products, matrix_product(): return jnp.dot(left, right, preferred_element_type=f32)  94.5 us
    dot_general x9, matrix products, through_rows(): lax.dot_general(left, right, (((1,), (1,)), ((), ())), preferred_element_...  90.7 us
    psum x1, waiting for transfers between devices, body(): grad_up = lax.psum(after(grad_up, grad_gate_ff), 'rep')  83.2 us
    ppermute x50, waiting for transfers between devices, hop(): return lax.ppermute(x, 'ctx', [(i, i ^ k) for i in range(C)])  83 us
    psum x1, waiting for transfers between devices, body(): grad_gate_ff = lax.psum(after(grad_gate_ff, grad_down), 'rep')  69.8 us
    unnamed x190, local copies, waits for them, and re-layouts  59.5 us
  transfers between devices with their start and end apart: 77, of which 30 were waited for; matrix products, arithmetic and copies ran while one was open for 36% of the time, Pallas kernels for 6%

profile of v1, /device:TPU:0, one launch (start us, length us, event | category | flops | bytes accessed | tf_op | source)
XLA Modules:
  0.0 1444.5 jit_solution(11617446387225424856)
XLA Ops:
  134.2 16.2 %collective-permute-done.18 = bf16[256,1536]{0,1:T(8,128)(2,1)S(1)} collective-permute-done((bf16[256,1536]{0,1:T(8,128)(2,1)S(1)}, bf16[256,1536]{0,1:T(8,128)(2,1)S(1)}, u32[]{:S(2)}, u32[]{:S(2)}) %collective-permute-start.18) | collective-permute-done | bytes 786464 | tf_op jit(solution)/shard_map/ppermute | solution.py:334
  156.1 14.7 %collective-permute-done.20 = bf16[256,1536]{0,1:T(8,128)(2,1)S(1)} collective-permute-done((bf16[256,1536]{0,1:T(8,128)(2,1)S(1)}, bf16[256,1536]{0,1:T(8,128)(2,1)S(1)}, u32[]{:S(2)}, u32[]{:S(2)}) %collective-permute-start.20) | collective-permute-done | bytes 786464 | tf_op jit(solution)/shard_map/ppermute | solution.py:334
  171.0 16.6 %collective-permute-done.22 = bf16[256,1536]{0,1:T(8,128)(2,1)S(1)} collective-permute-done((bf16[256,1536]{0,1:T(8,128)(2,1)S(1)}, bf16[256,1536]{0,1:T(8,128)(2,1)S(1)}, u32[]{:S(2)}, u32[]{:S(2)}) %collective-permute-start.22) | collective-permute-done | bytes 786464 | tf_op jit(solution)/shard_map/ppermute | solution.py:334
  187.8 16.2 %collective-permute-done.24 = bf16[256,1536]{0,1:T(8,128)(2,1)S(1)} collective-permute-done((bf16[256,1536]{0,1:T(8,128)(2,1)S(1)}, bf16[256,1536]{0,1:T(8,128)(2,1)S(1)}, u32[]{:S(2)}, u32[]{:S(2)}) %collective-permute-start.24) | collective-permute-done | bytes 786464 | tf_op jit(solution)/shard_map/ppermute | solution.py:334
  210.7 16.2 %fusion.2 = bf16[2048,2048]{1,0:T(8,128)(2,1)S(1)} fusion(f32[2048]{0:T(1024)S(1)} %bitcast.196, f32[2048]{0:T(1024)S(1)} %add_rsqrt_fusion, bf16[512,2048]{1,0:T(8,128)(2,1)S(1)} %collective-permute-done.2, bf16[512,2048]{1,0:T(8,128)(2,1)} %collective-permute-done.1, bf16[512,2048]{1,0:T(8,128)(2,1)S(1)} %collective-permute-done, ...), kind=kLoop, calls=%fused_computation.4 | loop fusion | flops 46137344 | bytes 16793600 | tf_op jit(solution)/shard_map/convert_element_type | solution.py:464
  228.6 17.1 %fusion.135.refs_2_ = f32[2048,1152]{1,0:T(8,128)} fusion(bf16[2048,2048]{1,0:T(8,128)(2,1)S(1)} %fusion.2, bf16[2048,1152]{0,1:T(8,128)(2,1)} %constant_dynamic-update-slice_fusion.24), kind=kOutput, calls=%fused_computation.330 | convolution fusion | flops 9663676416 | bytes 22544384 | tf_op jit(solution)/shard_map/dot_general | solution.py:32
  245.6 37.7 %attention_forward.1 = (bf16[2048,512]{1,0:T(8,128)(2,1)}, f32[2048,512]{1,0:T(8,128)}, f32[2048,128]{1,0:T(8,128)}) custom-call(s32[1]{0:T(128)} %bitcast.1.refs_0_, s32[8]{0:T(128)} %and_select_fusion.refs_1_, f32[2048,1152]{1,0:T(8,128)} %fusion.135.refs_2_, s32[2048,1]{1,0:T(8,128)} %iota_select_fusion.refs_3_, f32[1,128]{1,0:T(1,128)} %reshape.373.refs_4_, ...), custom_call_target="tpu_custom_call" | custom-call | flops 2147483648 | bytes 13631488 | tf_op jit(solution)/shard_map/attention_forward/pallas_call | solution.py:227
  320.9 71.3 %collective-permute-done.25 = bf16[256,1536]{0,1:T(8,128)(2,1)S(1)} collective-permute-done((bf16[256,1536]{0,1:T(8,128)(2,1)S(1)}, bf16[256,1536]{0,1:T(8,128)(2,1)S(1)}, u32[]{:S(2)}, u32[]{:S(2)}) %collective-permute-start.25) | collective-permute-done | bytes 786464 | tf_op jit(solution)/shard_map/ppermute | solution.py:334
  395.4 13.6 collective-permute-done.27
  409.2 16.6 %collective-permute-done.29 = bf16[256,1536]{0,1:T(8,128)(2,1)S(1)} collective-permute-done((bf16[256,1536]{0,1:T(8,128)(2,1)S(1)}, bf16[256,1536]{0,1:T(8,128)(2,1)S(1)}, u32[]{:S(2)}, u32[]{:S(2)}) %collective-permute-start.29) | collective-permute-done | bytes 786464 | tf_op jit(solution)/shard_map/ppermute | solution.py:334
  426.2 15.4 %collective-permute-done.31 = bf16[256,1536]{0,1:T(8,128)(2,1)S(1)} collective-permute-done((bf16[256,1536]{0,1:T(8,128)(2,1)S(1)}, bf16[256,1536]{0,1:T(8,128)(2,1)S(1)}, u32[]{:S(2)}, u32[]{:S(2)}) %collective-permute-start.31) | collective-permute-done | bytes 786464 | tf_op jit(solution)/shard_map/ppermute | solution.py:334
  471.1 16.9 %multiply_convert_fusion.3 = (bf16[1024,1536]{1,0:T(8,128)(2,1)S(1)}, bf16[1024,1536]{1,0:T(8,128)(2,1)}, bf16[1024,1536]{1,0:T(8,128)(2,1)}) fusion(f32[1024,1536]{1,0:T(8,128)} %fusion.118, f32[1024,1536]{1,0:T(8,128)} %fusion.23, bf16[2048,1536]{0,1:T(8,128)(2,1)} %copy-done.15, bf16[512,2048]{1,0:T(8,128)(2,1)S(1)} %collective-permute-done.17, ...), kind=kOutput, calls=%fused_computation.16 | convolution fusion | flops 6476005376 | bytes 32505856 | tf_op jit(solution)/shard_map/dot_general | solution.py:32
  578.7 15.4 %fusion.117 = f32[1024,1536]{1,0:T(8,128)} fusion(bf16[1024,2048]{1,0:T(8,128)(2,1)} %constant_dynamic-update-slice_fusion.40, bf16[768,2048]{1,0:T(8,128)(2,1)} %collective-permute-done.32, bf16[768,2048]{1,0:T(8,128)(2,1)} %convert_element_type.431, pred[]{:T(512)S(6)} %eq.20), kind=kOutput, calls=%fused_computation.313 | convolution fusion | flops 6470762496 | bytes 16777216 | tf_op jit(solution)/shard_map/dot_general | solution.py:40
  594.1 15.4 %multiply_convert_fusion.1 = (bf16[1024,1536]{1,0:T(8,128)(2,1)}, bf16[1024,1536]{1,0:T(8,128)(2,1)}, bf16[1024,1536]{1,0:T(8,128)(2,1)}) fusion(f32[1024,1536]{1,0:T(8,128)} %fusion.117, f32[1024,1536]{1,0:T(8,128)} %fusion.136, bf16[1024,2048]{1,0:T(8,128)(2,1)} %copy-done.36, bf16[2048,1536]{0,1:T(8,128)(2,1)S(1)} %bitcast.162), kind=kOutput, calls=%fused_computation.14 | convolution fusion | flops 6467616768 | bytes 32505856 | tf_op jit(solution)/shard_map/dot_general | solution.py:32
  702.8 37.6 %collective-permute-done.62 = bf16[768,2048]{1,0:T(8,128)(2,1)S(1)} collective-permute-done((bf16[768,2048]{1,0:T(8,128)(2,1)}, bf16[768,2048]{1,0:T(8,128)(2,1)S(1)}, u32[]{:S(2)}, u32[]{:S(2)}) %collective-permute-start.62) | collective-permute-done | bytes 3145760 | tf_op jit(solution)/shard_map/ppermute | solution.py:334
  748.4 58.3 %collective-permute-done.60 = bf16[1024,1536]{1,0:T(8,128)(2,1)} collective-permute-done((bf16[1024,1536]{1,0:T(8,128)(2,1)}, bf16[1024,1536]{1,0:T(8,128)(2,1)}, u32[]{:S(2)}, u32[]{:S(2)}) %collective-permute-start.60) | collective-permute-done | bytes 3145760 | tf_op jit(solution)/shard_map/ppermute | solution.py:334
  845.0 31.1 %collective-permute-done.61 = bf16[1024,1536]{1,0:T(8,128)(2,1)} collective-permute-done((bf16[1024,1536]{1,0:T(8,128)(2,1)}, bf16[1024,1536]{1,0:T(8,128)(2,1)}, u32[]{:S(2)}, u32[]{:S(2)}) %collective-permute-start.61) | collective-permute-done | bytes 3145760 | tf_op jit(solution)/shard_map/ppermute | solution.py:334
  889.3 56.1 %attention_backward.1 = (bf16[2048,1152]{1,0:T(8,128)(2,1)}, f32[8,128]{1,0:T(8,128)}) custom-call(s32[1]{0:T(128)} %bitcast.1.refs_0_, s32[8]{0:T(128)} %and_select_fusion.refs_1_, f32[2048,1152]{1,0:T(8,128)} %fusion.135.refs_2_, s32[2048,1]{1,0:T(8,128)} %iota_select_fusion.refs_3_, f32[1,128]{1,0:T(1,128)} %reshape.373.refs_4_, ...), custom_call_target="tpu_custom_call" | custom-call | flops 5368709120 | bytes 20447232 | tf_op jit(solution)/shard_map/attention_backward/pallas_call | solution.py:277
  1007.7 20.3 %collective-permute-done.49 = bf16[512,2048]{1,0:T(8,128)(2,1)} collective-permute-done((bf16[512,2048]{1,0:T(8,128)(2,1)}, bf16[512,2048]{1,0:T(8,128)(2,1)}, u32[]{:S(2)}, u32[]{:S(2)}) %collective-permute-start.49) | collective-permute-done | bytes 2097184 | tf_op jit(solution)/shard_map/ppermute | solution.py:331
  1042.2 69.8 %all-reduce.12.cloned.1.call-done = bf16[1024,1536]{1,0:T(8,128)(2,1)} async-done(((bf16[1024,1536]{1,0:T(8,128)(2,1)}), bf16[1024,1536]{1,0:T(8,128)(2,1)}) %all-reduce.12.cloned.1.call-update) | async-done | bytes 3145744 | tf_op jit(solution)/shard_map/psum | solution.py:525
  1152.0 83.2 %all-reduce.14.cloned.1.call-done = bf16[1024,1536]{1,0:T(8,128)(2,1)} async-done(((bf16[1024,1536]{1,0:T(8,128)(2,1)}), bf16[1024,1536]{1,0:T(8,128)(2,1)}) %all-reduce.14.cloned.1.call-update) | async-done | bytes 3145744 | tf_op jit(solution)/shard_map/psum | solution.py:527
  1242.7 46.2 %all-reduce.16.cloned.1.call-done = bf16[256,2048]{1,0:T(8,128)(2,1)} async-done(((bf16[256,2048]{1,0:T(8,128)(2,1)}), bf16[256,2048]{1,0:T(8,128)(2,1)}) %all-reduce.16.cloned.1.call-update) | async-done | bytes 1048592 | tf_op jit(solution)/shard_map/psum | solution.py:545
  1315.3 13.2 collective-permute-done.71
  1331.9 54.4 %all-reduce.18.cloned.1.call-done = bf16[1024,1152]{1,0:T(8,128)(2,1)} async-done(((bf16[1024,1152]{1,0:T(8,128)(2,1)}), bf16[1024,1152]{1,0:T(8,128)(2,1)}) %all-reduce.18.cloned.1.call-update) | async-done | bytes 2359312 | tf_op jit(solution)/shard_map/psum | solution.py:551
  (554 shorter events, 659.1 us)
Async XLA Ops:
  7.2 983.1 %all-reduce.10.cloned.1.call-start = ((), (), s32[]{:S(2)}) async-start(), calls=%async_computation | async-start | bytes 6291456 | tf_op jit(solution)/shard_map/psum | solution.py:523
  20.8 80.7 %collective-permute-start.1 = (bf16[512,2048]{1,0:T(8,128)(2,1)}, bf16[512,2048]{1,0:T(8,128)(2,1)}, u32[]{:S(2)}, u32[]{:S(2)}) collective-permute-start(bf16[512,2048]{1,0:T(8,128)(2,1)} %bitcast.145), channel_id=1, source_target_pairs={{0,2},{1,3},{2,0},{3,1},{4,6},{5,7},{6,4},{7,5},{8,10},{9,11},{10,... | collective-permute-start | bytes 6291464 | tf_op jit(solution)/shard_map/ppermute | solution.py:331
  304.3 143.5 %collective-permute-start.32 = (bf16[768,2048]{1,0:T(8,128)(2,1)S(1)}, bf16[768,2048]{1,0:T(8,128)(2,1)}, u32[]{:S(2)}, u32[]{:S(2)}) collective-permute-start(bf16[768,2048]{1,0:T(8,128)(2,1)S(1)} %copy-done.22), channel_id=1, source_target_pairs={{0,4},{4,0},{1,5},{5,1},{2,6},{6,2},{3,7},{7,3},{8,12},{12,8},{9,1... | collective-permute-start | bytes 9437192 | tf_op jit(solution)/shard_map/ppermute | solution.py:334
  307.5 84.6 %collective-permute-start.25 = (bf16[256,1536]{0,1:T(8,128)(2,1)S(1)}, bf16[256,1536]{0,1:T(8,128)(2,1)S(1)}, u32[]{:S(2)}, u32[]{:S(2)}) collective-permute-start(bf16[256,1536]{0,1:T(8,128)(2,1)S(1)} %bitcast.168), channel_id=1, source_target_pairs={{0,4},{4,0},{1,5},{5,1},{2,6},{6,2},{3,7},{7,3},{8,12},{12,8},{9,1... | collective-permute-start | bytes 2359304 | tf_op jit(solution)/shard_map/ppermute | solution.py:334
  310.8 82.3 %collective-permute-start.28 = (bf16[256,1536]{0,1:T(8,128)(2,1)S(1)}, bf16[256,1536]{0,1:T(8,128)(2,1)S(1)}, u32[]{:S(2)}, u32[]{:S(2)}) collective-permute-start(bf16[256,1536]{0,1:T(8,128)(2,1)S(1)} %bitcast.179), channel_id=1, source_target_pairs={{0,2},{1,3},{2,0},{3,1},{4,6},{5,7},{6,4},{7,5},{8,10},{9,11},{10,... | collective-permute-start | bytes 2359304 | tf_op jit(solution)/shard_map/ppermute | solution.py:331
  312.4 82.3 %collective-permute-start.30 = (bf16[256,1536]{0,1:T(8,128)(2,1)S(1)}, bf16[256,1536]{0,1:T(8,128)(2,1)S(1)}, u32[]{:S(2)}, u32[]{:S(2)}) collective-permute-start(bf16[256,1536]{0,1:T(8,128)(2,1)S(1)} %bitcast.178), channel_id=1, source_target_pairs={{0,3},{1,2},{2,1},{3,0},{4,7},{5,6},{6,5},{7,4},{8,11},{9,10},{10,... | collective-permute-start | bytes 2359304 | tf_op jit(solution)/shard_map/ppermute | solution.py:331
  312.5 96.6 %collective-permute-start.27 = (bf16[256,1536]{0,1:T(8,128)(2,1)S(1)}, bf16[256,1536]{0,1:T(8,128)(2,1)S(1)}, u32[]{:S(2)}, u32[]{:S(2)}) collective-permute-start(bf16[256,1536]{0,1:T(8,128)(2,1)S(1)} %collective-permute-done.26), channel_id=1, source_target_pairs={{0,4},{4,0},{1,5},{5,1},{2,6},{6,2},{3,7},{7,3},{8,12},{12,8},{9,1... | collective-permute-start | bytes 2359304 | tf_op jit(solution)/shard_map/ppermute | solution.py:334
  441.7 82.6 %collective-permute-start.40 = (bf16[512,2048]{1,0:T(8,128)(2,1)}, bf16[512,2048]{1,0:T(8,128)(2,1)}, u32[]{:S(2)}, u32[]{:S(2)}) collective-permute-start(bf16[512,2048]{1,0:T(8,128)(2,1)} %fusion.22), channel_id=1, source_target_pairs={{0,2},{1,3},{2,0},{3,1},{4,6},{5,7},{6,4},{7,5},{8,10},{9,11},{10,... | collective-permute-start | bytes 6291464 | tf_op jit(solution)/shard_map/ppermute | solution.py:331
  443.4 90.2 %collective-permute-start.34 = (bf16[512,2048]{1,0:T(8,128)(2,1)S(1)}, bf16[512,2048]{1,0:T(8,128)(2,1)}, u32[]{:S(2)}, u32[]{:S(2)}) collective-permute-start(bf16[512,2048]{1,0:T(8,128)(2,1)S(1)} %multiply_convert_fusion.6), channel_id=1, source_target_pairs={{0,2},{1,3},{2,0},{3,1},{4,6},{5,7},{6,4},{7,5},{8,10},{9,11},{10,... | collective-permute-start | bytes 6291464 | tf_op jit(solution)/shard_map/ppermute | solution.py:331
  511.5 306.0 %collective-permute-start.39 = (bf16[512,2048]{1,0:T(8,128)(2,1)}, bf16[512,2048]{1,0:T(8,128)(2,1)}, u32[]{:S(2)}, u32[]{:S(2)}) collective-permute-start(bf16[512,2048]{1,0:T(8,128)(2,1)} %slice.486), channel_id=1, source_target_pairs={{0,1},{1,0},{2,3},{3,2},{4,5},{5,4},{6,7},{7,6},{8,9},{9,8},{10,11... | collective-permute-start | bytes 6291464 | tf_op jit(solution)/shard_map/ppermute | solution.py:331
  677.7 129.1 %collective-permute-start.60 = (bf16[1024,1536]{1,0:T(8,128)(2,1)}, bf16[1024,1536]{1,0:T(8,128)(2,1)}, u32[]{:S(2)}, u32[]{:S(2)}) collective-permute-start(bf16[1024,1536]{1,0:T(8,128)(2,1)} %add_convert_fusion.5), channel_id=1, source_target_pairs={{0,4},{4,0},{1,5},{5,1},{2,6},{6,2},{3,7},{7,3},{8,12},{12,8},{9,1... | collective-permute-start | bytes 9437192 | tf_op jit(solution)/shard_map/ppermute | solution.py:334
  693.2 130.4 %collective-permute-start.33 = (bf16[512,2048]{1,0:T(8,128)(2,1)}, bf16[512,2048]{1,0:T(8,128)(2,1)}, u32[]{:S(2)}, u32[]{:S(2)}) collective-permute-start(bf16[512,2048]{1,0:T(8,128)(2,1)} %slice.488), channel_id=1, source_target_pairs={{0,1},{1,0},{2,3},{3,2},{4,5},{5,4},{6,7},{7,6},{8,9},{9,8},{10,11... | collective-permute-start | bytes 6291464 | tf_op jit(solution)/shard_map/ppermute | solution.py:331
  697.1 120.3 %collective-permute-start.43 = (bf16[512,2048]{1,0:T(8,128)(2,1)}, bf16[512,2048]{1,0:T(8,128)(2,1)S(1)}, u32[]{:S(2)}, u32[]{:S(2)}) collective-permute-start(bf16[512,2048]{1,0:T(8,128)(2,1)} %fusion.15), channel_id=1, source_target_pairs={{0,2},{1,3},{2,0},{3,1},{4,6},{5,7},{6,4},{7,5},{8,10},{9,11},{10,... | collective-permute-start | bytes 6291464 | tf_op jit(solution)/shard_map/ppermute | solution.py:331
  740.4 83.2 %collective-permute-start.37 = (bf16[512,2048]{1,0:T(8,128)(2,1)}, bf16[512,2048]{1,0:T(8,128)(2,1)}, u32[]{:S(2)}, u32[]{:S(2)}) collective-permute-start(bf16[512,2048]{1,0:T(8,128)(2,1)} %fusion.17), channel_id=1, source_target_pairs={{0,2},{1,3},{2,0},{3,1},{4,6},{5,7},{6,4},{7,5},{8,10},{9,11},{10,... | collective-permute-start | bytes 6291464 | tf_op jit(solution)/shard_map/ppermute | solution.py:331
  748.4 363.6 %all-reduce.12.cloned.1.call-start = ((), (), s32[]{:S(2)}) async-start(), calls=%async_computation.1 | async-start | bytes 6291456 | tf_op jit(solution)/shard_map/psum | solution.py:525
  883.3 103.7 %collective-permute-start.56 = (bf16[512,2048]{1,0:T(8,128)(2,1)S(1)}, bf16[512,2048]{1,0:T(8,128)(2,1)}, u32[]{:S(2)}, u32[]{:S(2)}) collective-permute-start(bf16[512,2048]{1,0:T(8,128)(2,1)S(1)} %get-tuple-element.63), channel_id=1, source_target_pairs={{0,1},{1,0},{2,3},{3,2},{4,5},{5,4},{6,7},{7,6},{8,9},{9,8},{10,11... | collective-permute-start | bytes 6291464 | tf_op jit(solution)/shard_map/ppermute | solution.py:331
  883.4 103.7 %collective-permute-start.57 = (bf16[512,2048]{1,0:T(8,128)(2,1)S(1)}, bf16[512,2048]{1,0:T(8,128)(2,1)}, u32[]{:S(2)}, u32[]{:S(2)}) collective-permute-start(bf16[512,2048]{1,0:T(8,128)(2,1)S(1)} %get-tuple-element.63), channel_id=1, source_target_pairs={{0,2},{1,3},{2,0},{3,1},{4,6},{5,7},{6,4},{7,5},{8,10},{9,11},{10,... | collective-permute-start | bytes 6291464 | tf_op jit(solution)/shard_map/ppermute | solution.py:331
  990.3 245.0 %all-reduce.14.cloned.1.call-start = ((), (), s32[]{:S(2)}) async-start(), calls=%async_computation.2 | async-start | bytes 6291456 | tf_op jit(solution)/shard_map/psum | solution.py:527
  1037.5 74.6 %collective-permute-start.51 = (f32[34,128]{1,0:T(8,128)S(1)}, f32[34,128]{1,0:T(8,128)S(1)}, u32[]{:S(2)}, u32[]{:S(2)}) collective-permute-start(f32[34,128]{1,0:T(8,128)S(1)} %fusion.108), channel_id=1, source_target_pairs={{0,2},{1,3},{2,0},{3,1},{4,6},{5,7},{6,4},{7,5},{8,10},{9,11},{10,... | collective-permute-start | bytes 52232 | tf_op jit(solution)/shard_map/ppermute | solution.py:331
  1112.0 176.9 %all-reduce.16.cloned.1.call-start = ((), (), s32[]{:S(2)}) async-start(), calls=%async_computation.3 | async-start | bytes 2097152 | tf_op jit(solution)/shard_map/psum | solution.py:545
  1133.1 102.3 %collective-permute-start.66 = (bf16[256,1536]{1,0:T(8,128)(2,1)}, bf16[256,1536]{1,0:T(8,128)(2,1)}, u32[]{:S(2)}, u32[]{:S(2)}) collective-permute-start(bf16[256,1536]{1,0:T(8,128)(2,1)} %get-tuple-element.90), channel_id=1, source_target_pairs={{0,1},{1,0},{2,3},{3,2},{4,5},{5,4},{6,7},{7,6},{8,9},{9,8},{10,11... | collective-permute-start | bytes 2359304 | tf_op jit(solution)/shard_map/ppermute | solution.py:331
  1133.1 106.3 %collective-permute-start.67 = (bf16[256,1536]{1,0:T(8,128)(2,1)}, bf16[256,1536]{1,0:T(8,128)(2,1)}, u32[]{:S(2)}, u32[]{:S(2)}) collective-permute-start(bf16[256,1536]{1,0:T(8,128)(2,1)} %get-tuple-element.89), channel_id=1, source_target_pairs={{0,2},{1,3},{2,0},{3,1},{4,6},{5,7},{6,4},{7,5},{8,10},{9,11},{10,... | collective-permute-start | bytes 2359304 | tf_op jit(solution)/shard_map/ppermute | solution.py:331
  1144.8 146.1 %collective-permute-start.68 = (bf16[256,1536]{1,0:T(8,128)(2,1)}, bf16[256,1536]{1,0:T(8,128)(2,1)}, u32[]{:S(2)}, u32[]{:S(2)}) collective-permute-start(bf16[256,1536]{1,0:T(8,128)(2,1)} %get-tuple-element.88), channel_id=1, source_target_pairs={{0,3},{1,2},{2,1},{3,0},{4,7},{5,6},{6,5},{7,4},{8,11},{9,10},{10,... | collective-permute-start | bytes 2359304 | tf_op jit(solution)/shard_map/ppermute | solution.py:331
  1235.3 151.0 %all-reduce.18.cloned.1.call-start = ((), (), s32[]{:S(2)}) async-start(), calls=%async_computation.4 | async-start | bytes 4718592 | tf_op jit(solution)/shard_map/psum | solution.py:551
  (138 other events, 3918.5 us)
Sparse Core Ops, SparseCore 0:
  748.5 121.3 all-reduce.9
  990.4 121.5 all-reduce.11
  1114.4 120.8 all-reduce.13
  1238.0 50.8 all-reduce.15
  1291.2 94.9 all-reduce.17
